TPU v7x, 128 devices: a whole 4x4x4 slice. The times are simulated.
128 devices in a mesh: dp: 4 (over y), expert: 32 (over x, z, core).
Axes of the slice: x: 4, y: 4, z: 4, core: 2. Of those that a mesh axis runs over, the one named last changes fastest.
Arguments:
- tokens: bfloat16 [8192, 4096], P(('dp', 'expert')), may hold values from -6 to 6
- routes: int32 [8192, 8], P(('dp', 'expert')), may hold values from 0 to 63, all different within a row; in each aligned block of 64 rows (0 to 63, 64 to 127, ...) at most 12 rows name the same one
- gate_fixed: int32 [8192, 8], P(('dp', 'expert')), may hold values from 1 to 65535
- w_gate: bfloat16 [128, 4096, 768], P(('dp', 'expert')), may hold values from -0.09375 to 0.09375
- w_up: bfloat16 [128, 4096, 768], P(('dp', 'expert')), may hold values from -0.09375 to 0.09375
- w_down: bfloat16 [128, 768, 4096], P(('dp', 'expert')), may hold values from -0.15625 to 0.15625
Outputs:
- mixed: bfloat16 [8192, 4096], P(('dp', 'expert'))
Inputs may be any that keep to these rules, and one draw needn't show every extreme that they name: `routes`: each row names 8 different experts. In each aligned block of 64 rows (the rows of one device) no expert is named by more than 12 rows, and in some block one expert is named by exactly 12 rows.
All inputs are finite; a program needn't handle non-finite values.
Results may differ from a plain program's by a relative error of at most 0.0058.
Values may be sent and summed in bfloat16 or wider, within the bound.
A program may use at most 192 MiB of HBM per device.

v0:
```python
import jax
import jax.numpy as jnp
from jax import lax
from jax.experimental import pallas as pl
from jax.experimental.pallas import tpu as pltpu
from jax.sharding import PartitionSpec as P

MESH = pl.DeviceIdType.MESH
F32 = jnp.float32
BF16 = jnp.bfloat16

SIDE = 4
TOK = 64
TOP = 8
EXPERTS = 64
WIDTH = 4096
HALF = 768
GROUPS = 3
SLOTS = 4
BLOCK = SIDE * SLOTS
ROWS = SIDE * SIDE * BLOCK

PARTS = ((0, 1408), (1408, 1408), (2816, 1280))
ORDERS = ("yxz", "xzy", "zyx")
STEPS = (1, 3, 2)
CHUNK = 256


def nt(left, right):
    return lax.dot_general(left, right, (((1,), (1,)), ((), ())), preferred_element_type=F32)


def iota(shape, dim):
    return lax.broadcasted_iota(jnp.int32, shape, dim)


def ones_where(condition):
    return jnp.where(condition, 1.0, 0.0).astype(BF16)


def cols(part):
    return pl.ds(PARTS[part][0], PARTS[part][1])


def turn_matrix(forward):
    row = iota((ROWS, ROWS), 0)
    if forward:
        source = ((row >> 2) & 3) * 64 + (row >> 6) * 16 + ((row >> 4) & 3) * 4 + (row & 3)
    else:
        source = ((row >> 4) & 3) * 64 + ((row >> 2) & 3) * 16 + (row >> 6) * 4 + (row & 3)
    return ones_where(source == iota((ROWS, ROWS), 1))


def kernel(
    x_ref,
    routes_ref,
    gate_ref,
    wg_hbm,
    wu_hbm,
    wd_hbm,
    sums,
    mid_ref,
    back_ref,
    home_ref,
    lines,
    tables,
    packed,
    landed,
    hidden,
    turned,
    mixes,
    mixed,
    wg,
    wu,
    wd,
    sem_send,
    sem_recv,
    end_send,
    end_recv,
    tab_send,
    tab_recv,
    w_send,
    w_recv,
    w_local,
    own_sem,
    load_sem,
    x_sem,
):
    row = lax.axis_index("expert")
    at = {"y": lax.axis_index("dp"), "x": row // 8, "z": (row // 2) % 4}
    core = row % 2

    def device(where, which):
        return (where["y"], (where["x"] * 4 + where["z"]) * 2 + which)

    def peer(axis, shift):
        where = dict(at)
        where[axis] = (at[axis] + shift) % SIDE
        return device(where, core)

    partner = device(at, 1 - core)

    barrier = pltpu.get_barrier_semaphore()
    for step in (2, 1, 3):
        for axis in "yxz":
            pl.semaphore_signal(barrier, inc=1, device_id=peer(axis, step), device_id_type=MESH)
    pl.semaphore_signal(barrier, inc=1, device_id=partner, device_id_type=MESH)

    own_rows = pltpu.make_async_copy(x_ref, lines.at[pl.ds(0, TOK)], x_sem.at[0])
    own_rows.start()
    own_weights = [
        pltpu.make_async_copy(src.at[0], dst.at[0], w_local.at[index])
        for index, (src, dst) in enumerate(((wg_hbm, wg), (wu_hbm, wu), (wd_hbm, wd)))
    ]

    quant = gate_ref[...].astype(F32)
    weight = quant / jnp.sum(quant, axis=0, keepdims=True)
    named = jnp.zeros((EXPERTS, TOK), F32)
    share = jnp.zeros((EXPERTS, TOK), F32)
    for k in range(TOP):
        hit = routes_ref[k : k + 1, :] == iota((EXPERTS, TOK), 0)
        named = named + jnp.where(hit, 1.0, 0.0)
        share = share + jnp.where(hit, weight[k : k + 1, :], 0.0)
    earlier = ones_where(iota((TOK, TOK), 0) < iota((TOK, TOK), 1))
    before = jnp.dot(named.astype(BF16), earlier, preferred_element_type=F32)
    slots = jnp.where(named > 0.5, before, -1.0)
    own_table = jnp.concatenate([slots, share], axis=0).T.astype(BF16)
    for part in range(3):
        tables[part, 0:TOK, :] = own_table

    pl.semaphore_wait(barrier, 10)

    def phase0(part, step):
        return pltpu.make_async_remote_copy(
            src_ref=x_ref.at[:, cols(part)],
            dst_ref=lines.at[pl.ds(step * TOK, TOK), cols(part)],
            send_sem=end_send.at[0, part, step],
            recv_sem=end_recv.at[0, part, step],
            device_id=peer(ORDERS[part][0], -step),
            device_id_type=MESH,
        )

    def table_copy(part, step):
        return pltpu.make_async_remote_copy(
            src_ref=tables.at[part, pl.ds(0, TOK)],
            dst_ref=tables.at[part, pl.ds(step * TOK, TOK)],
            send_sem=tab_send.at[part, step],
            recv_sem=tab_recv.at[part, step],
            device_id=peer(ORDERS[part][0], -step),
            device_id_type=MESH,
        )

    for step in STEPS:
        for part in range(3):
            table_copy(part, step).start()
    for step in STEPS:
        for part in range(3):
            phase0(part, step).start()

    other_weights = [
        pltpu.make_async_remote_copy(
            src_ref=src.at[0],
            dst_ref=dst.at[1],
            send_sem=w_send.at[index],
            recv_sem=w_recv.at[index],
            device_id=partner,
            device_id_type=MESH,
        )
        for index, (src, dst) in enumerate(((wg_hbm, wg), (wu_hbm, wu), (wd_hbm, wd)))
    ]
    for copy in own_weights + other_weights:
        copy.start()

    def chosen(part):
        index = iota((ROWS, EXPERTS), 0)
        a, b, c = (at[axis] for axis in ORDERS[part])
        where = dict(zip(ORDERS[part], (a, (b - (index >> 6)) & 3, (c - ((index >> 4) & 3)) & 3)))
        expert = where["y"] * 16 + where["x"] * 4 + where["z"]
        return ones_where(expert == iota((ROWS, EXPERTS), 1))

    def sends(phase, group, part, step, src, dst, target):
        return pltpu.make_async_remote_copy(
            src_ref=src,
            dst_ref=dst,
            send_sem=sem_send.at[phase, group, part, step],
            recv_sem=sem_recv.at[phase, group, part, step],
            device_id=target,
            device_id_type=MESH,
        )

    def hop(phase, group, part, step):
        order = ORDERS[part]
        here = cols(part)
        if phase == 0:
            src, dst = packed.at[group, step, :, :, here], mid_ref.at[group, :, step, :, here]
            target = (order[1], -step)
        elif phase == 1:
            src, dst = mid_ref.at[group, step, :, :, here], landed.at[group, step, :, :, here]
            target = (order[2], -step)
        elif phase == 2:
            src, dst = landed.at[group, step, :, :, here], back_ref.at[group, :, step, :, here]
            target = (order[2], step)
        else:
            src, dst = back_ref.at[group, step, :, :, here], home_ref.at[group, step, :, :, here]
            target = (order[1], step)
        if step == 0:
            if phase == 3:
                dst = packed.at[group, 0, :, :, here]
            return pltpu.make_async_copy(src, dst, own_sem.at[phase, group, part])
        return sends(phase, group, part, step, src, dst, peer(*target))

    def start(phase, group, part):
        for step in STEPS + (0,):
            hop(phase, group, part, step).start()

    def finish(phase, group, part):
        for step in (0,) + STEPS:
            hop(phase, group, part, step).wait()

    def start_all(phase, group):
        for step in STEPS + (0,):
            for part in range(3):
                hop(phase, group, part, step).start()

    def finish_all(phase, group):
        for part in range(3):
            finish(phase, group, part)

    def gather(group, part):
        first, size = PARTS[part]
        found = nt(chosen(part), tables[part, :, 0:EXPERTS])
        row = iota((ROWS, SIDE * TOK), 0)
        slot = (row & 3) + group * SLOTS
        holder = iota((ROWS, SIDE * TOK), 1) >> 6
        pick = ones_where((found == slot.astype(F32)) & (holder == ((row >> 2) & 3)))
        rows = jnp.dot(pick, lines[:, first : first + size], preferred_element_type=F32)
        packed[group, :, :, :, first : first + size] = rows.astype(BF16).reshape(SIDE, SIDE, BLOCK, size)

    def mix_tables(part):
        select = chosen(part)
        found = nt(tables[part, :, 0:EXPERTS], select)
        scale = nt(tables[part, :, EXPERTS : 2 * EXPERTS], select)
        col = iota((SIDE * TOK, ROWS), 1)
        mine = (iota((SIDE * TOK, ROWS), 0) >> 6) == ((col >> 2) & 3)
        for group in range(GROUPS):
            slot = (col & 3) + group * SLOTS
            mixes[group, part] = jnp.where((found == slot.astype(F32)) & mine, scale, 0.0).astype(BF16)

    own_rows.wait()
    for part in range(3):
        for step in STEPS:
            table_copy(part, step).wait()
    for part in range(3):
        for step in STEPS:
            phase0(part, step).wait()
        gather(0, part)
        start(0, 0, part)
    for part in range(3):
        gather(1, part)
        start(0, 1, part)
    for part in range(3):
        gather(2, part)
    for part in range(3):
        finish(0, 0, part)
        start(1, 0, part)
    for part in range(3):
        start(0, 2, part)
    for part in range(3):
        mix_tables(part)
    for part in range(3):
        finish(0, 1, part)
        start(1, 1, part)

    def arrange(group):
        for part in range(3):
            first, size = PARTS[part]
            rows = landed[group, :, :, :, first : first + size]
            if part:
                rows = rows.reshape(ROWS, size)
                rows = jnp.dot(turn_matrix(part == 1), rows, preferred_element_type=F32)
                rows = rows.astype(BF16).reshape(SIDE, SIDE, BLOCK, size)
            packed[group, :, :, :, first : first + size] = rows

    def inner(group):
        @pl.loop(0, 2 * HALF // CHUNK)
        def _(index):
            side = index // (HALF // CHUNK)
            these = pl.ds(pl.multiple_of((index % (HALF // CHUNK)) * CHUNK, CHUNK), CHUNK)
            those = pl.ds(pl.multiple_of(index * CHUNK, CHUNK), CHUNK)
            rows = packed[group].reshape(ROWS, WIDTH)
            gate = jnp.dot(rows, wg[side, :, these], preferred_element_type=F32)
            upper = jnp.dot(rows, wu[side, :, these], preferred_element_type=F32)
            hidden[:, those] = (gate / (1.0 + jnp.exp(-gate)) * upper).astype(BF16)

    def outer(group, part):
        first, size = PARTS[part]
        source = hidden
        if part:
            turned[...] = jnp.dot(
                turn_matrix(part == 2), hidden[...], preferred_element_type=F32
            ).astype(BF16)
            source = turned
        for begin in range(first, first + size, CHUNK):
            end = min(begin + CHUNK, first + size)
            total = jnp.dot(source[:, :HALF], wd[0, :, begin:end], preferred_element_type=F32)
            total = total + jnp.dot(source[:, HALF:], wd[1, :, begin:end], preferred_element_type=F32)
            landed[group, :, :, :, begin:end] = total.astype(BF16).reshape(SIDE, SIDE, BLOCK, end - begin)

    for copy in own_weights + other_weights:
        copy.wait()

    for group in range(GROUPS):
        finish_all(1, group)
        arrange(group)
        inner(group)
        if group == 0:
            for part in range(3):
                finish(0, 2, part)
                start(1, 2, part)
        else:
            for part in range(3):
                finish(2, group - 1, part)
                start(3, group - 1, part)
        for part in range(3):
            outer(group, part)
            start(2, group, part)

    def load(group, part, step):
        return pltpu.make_async_copy(
            home_ref.at[group, step, :, :, cols(part)],
            packed.at[group, step, :, :, cols(part)],
            load_sem.at[group, part, step],
        )

    def bring(group, part):
        finish(3, group, part)
        for step in STEPS:
            load(group, part, step).start()

    def mix(group, part):
        first, size = PARTS[part]
        for step in STEPS:
            load(group, part, step).wait()
        rows = packed[group, :, :, :, first : first + size].reshape(ROWS, size)
        total = jnp.dot(mixes[group, part], rows, preferred_element_type=F32)
        if group:
            total = total + mixed[:, first : first + size]
        if group == GROUPS - 1:
            lines[:, first : first + size] = total.astype(BF16)
        else:
            mixed[:, first : first + size] = total

    def phase5(part, step):
        src = lines.at[pl.ds(step * TOK, TOK), cols(part)]
        dst = sums.at[step, :, cols(part)]
        if step == 0:
            return pltpu.make_async_copy(src, dst, x_sem.at[1 + part])
        return pltpu.make_async_remote_copy(
            src_ref=src,
            dst_ref=dst,
            send_sem=end_send.at[1, part, step],
            recv_sem=end_recv.at[1, part, step],
            device_id=peer(ORDERS[part][0], step),
            device_id_type=MESH,
        )

    for part in range(3):
        bring(0, part)
    for part in range(3):
        mix(0, part)
    for part in range(3):
        finish(2, 2, part)
        start(3, 2, part)
    for part in range(3):
        bring(1, part)
    for part in range(3):
        mix(1, part)
    for part in range(3):
        bring(2, part)
        mix(2, part)
        for step in STEPS + (0,):
            phase5(part, step).start()
    for part in range(3):
        for step in STEPS + (0,):
            phase5(part, step).wait()


def on_device(tokens, routes, gate_fixed, w_gate, w_up, w_down):
    big = jax.ShapeDtypeStruct((GROUPS, SIDE, SIDE, BLOCK, WIDTH), BF16)
    vmem = pl.BlockSpec(memory_space=pltpu.VMEM)
    hbm = pl.BlockSpec(memory_space=pltpu.HBM)
    dma = pltpu.SemaphoreType.DMA
    sums, _, _, _ = pl.pallas_call(
        kernel,
        out_shape=(jax.ShapeDtypeStruct((SIDE, TOK, WIDTH), BF16), big, big, big),
        in_specs=[hbm, vmem, vmem, hbm, hbm, hbm],
        out_specs=(hbm, hbm, hbm, hbm),
        scratch_shapes=[
            pltpu.VMEM((SIDE * TOK, WIDTH), BF16),
            pltpu.VMEM((3, SIDE * TOK, 2 * EXPERTS), BF16),
            pltpu.VMEM((GROUPS, SIDE, SIDE, BLOCK, WIDTH), BF16),
            pltpu.VMEM((GROUPS, SIDE, SIDE, BLOCK, WIDTH), BF16),
            pltpu.VMEM((ROWS, 2 * HALF), BF16),
            pltpu.VMEM((ROWS, 2 * HALF), BF16),
            pltpu.VMEM((GROUPS, 3, SIDE * TOK, ROWS), BF16),
            pltpu.VMEM((SIDE * TOK, WIDTH), F32),
            pltpu.VMEM((2, WIDTH, HALF), BF16),
            pltpu.VMEM((2, WIDTH, HALF), BF16),
            pltpu.VMEM((2, HALF, WIDTH), BF16),
            dma((4, GROUPS, 3, SIDE)),
            dma((4, GROUPS, 3, SIDE)),
            dma((2, 3, SIDE)),
            dma((2, 3, SIDE)),
            dma((3, SIDE)),
            dma((3, SIDE)),
            dma((3,)),
            dma((3,)),
            dma((3,)),
            dma((4, GROUPS, 3)),
            dma((GROUPS, 3, SIDE)),
            dma((4,)),
        ],
        compiler_params=pltpu.CompilerParams(
            collective_id=0, has_side_effects=True, vmem_limit_bytes=67043328
        ),
        name="moe",
    )(tokens, routes.T, gate_fixed.T, w_gate, w_up, w_down)
    return jnp.sum(sums.astype(F32), axis=0).astype(BF16)


def solution(mesh):
    split = P(("dp", "expert"), None)
    placed = (split, split, split) + (P(("dp", "expert"), None, None),) * 3
    return jax.shard_map(on_device, mesh=mesh, in_specs=placed, out_specs=split, check_vma=False)
```

profile of v0, /device:TPU:0, one launch (start us, length us, event | category | flops | bytes accessed | tf_op | source)
XLA Modules:
  0.0 134.3 jit_solution(273520319515363544)
XLA Ops:
  0.0 131.4 %moe.1 = (bf16[4,64,4096]{2,1,0:T(8,128)(2,1)}, bf16[3,4,4,16,4096]{4,3,2,1,0:T(8,128)(2,1)}, bf16[3,4,4,16,4096]{4,3,2,1,0:T(8,128)(2,1)}, bf16[3,4,4,16,4096]{4,3,2,1,0:T(8,128)(2,1)}) custom-call(bf16[64,4096]{1,0:T(8,128)(2,1)} %x_ref.1, s32[8,64]{1,0:T(8,128)} %bitcast.2, s32[8,64]{1,0:T(8,128)} %bitcast.3, bf16[1,4096,768]{2,1,0:T(8,128)(2,1)} %wg_hbm.1, ...), custom_call_target="tpu_custom_call" | custom-call | tf_op jit(solution)/shard_map/moe/pallas_call | solution.py:393
  131.4 2.9 %reduce_sum.12 = bf16[64,4096]{1,0:T(8,128)(2,1)} reduce(bf16[4,64,4096]{2,1,0:T(8,128)(2,1)} %get-tuple-element.6, bf16[]{:T(256)} %constant.2.clone.1), dimensions={0}, to_apply=%region_0.0 | reduce | flops 786432 | bytes 2621442 | tf_op jit(solution)/shard_map/reduce_sum | solution.py:428
where the time goes:
time: 135 us; the launch traced here: 134 us
  Pallas kernels  131 us (97%)
  other arithmetic  2.86 us (2%)
    pallas_call x1, Pallas kernels, on_device(): pl.pallas_call(kernel, out_shape=(jax.ShapeDtypeStruct((SIDE, TOK, WIDTH)...  131 us
    reduce_sum x1, other arithmetic, on_device(): return jnp.sum(sums.astype(F32), axis=0).astype(BF16)  2.86 us

commit v1 on v0

--- a/solution.py
+++ b/solution.py
@@ -21,6 +21,7 @@
 ROWS = SIDE * SIDE * BLOCK
 
 PARTS = ((0, 1408), (1408, 1408), (2816, 1280))
+BACK_PARTS = ((0, 1280), (1280, 1408), (2688, 1408))
 ORDERS = ("yxz", "xzy", "zyx")
 STEPS = (1, 3, 2)
 CHUNK = 256
@@ -40,6 +41,19 @@
 
 def cols(part):
     return pl.ds(PARTS[part][0], PARTS[part][1])
+
+
+def back_cols(part):
+    return pl.ds(BACK_PARTS[part][0], BACK_PARTS[part][1])
+
+
+RELAYED = {1: 0, 3: 1}
+
+
+def half_cols(parts, part, half):
+    first, size = parts[part]
+    cut = 640
+    return pl.ds(first + half * cut, size - cut if half else cut)
 
 
 def turn_matrix(forward):
@@ -63,6 +77,7 @@
     back_ref,
     home_ref,
     lines,
+    passing,
     tables,
     packed,
     landed,
@@ -75,6 +90,8 @@
     wd,
     sem_send,
     sem_recv,
+    start_send,
+    start_recv,
     end_send,
     end_recv,
     tab_send,
@@ -101,7 +118,7 @@
     partner = device(at, 1 - core)
 
     barrier = pltpu.get_barrier_semaphore()
-    for step in (2, 1, 3):
+    for step in (1, 3):
         for axis in "yxz":
             pl.semaphore_signal(barrier, inc=1, device_id=peer(axis, step), device_id_type=MESH)
     pl.semaphore_signal(barrier, inc=1, device_id=partner, device_id_type=MESH)
@@ -128,34 +145,48 @@
     for part in range(3):
         tables[part, 0:TOK, :] = own_table
 
-    pl.semaphore_wait(barrier, 10)
-
-    def phase0(part, step):
+    pl.semaphore_wait(barrier, 7)
+
+    def phase0(part, step, half):
+        here = half_cols(PARTS, part, half)
         return pltpu.make_async_remote_copy(
-            src_ref=x_ref.at[:, cols(part)],
-            dst_ref=lines.at[pl.ds(step * TOK, TOK), cols(part)],
-            send_sem=end_send.at[0, part, step],
-            recv_sem=end_recv.at[0, part, step],
+            src_ref=x_ref.at[:, here],
+            dst_ref=lines.at[pl.ds(step * TOK, TOK), here],
+            send_sem=start_send.at[half, part, step],
+            recv_sem=start_recv.at[half, part, step],
             device_id=peer(ORDERS[part][0], -step),
             device_id_type=MESH,
         )
 
+    def relay0(part, step):
+        here = half_cols(PARTS, part, RELAYED[step])
+        return pltpu.make_async_remote_copy(
+            src_ref=lines.at[pl.ds(step * TOK, TOK), here],
+            dst_ref=lines.at[pl.ds(2 * TOK, TOK), here],
+            send_sem=start_send.at[2, part, step],
+            recv_sem=start_recv.at[2, part, step],
+            device_id=peer(ORDERS[part][0], -step),
+            device_id_type=MESH,
+        )
+
     def table_copy(part, step):
+        origin = 1 if step == 2 else 0
         return pltpu.make_async_remote_copy(
-            src_ref=tables.at[part, pl.ds(0, TOK)],
+            src_ref=tables.at[part, pl.ds(origin * TOK, TOK)],
             dst_ref=tables.at[part, pl.ds(step * TOK, TOK)],
             send_sem=tab_send.at[part, step],
             recv_sem=tab_recv.at[part, step],
-            device_id=peer(ORDERS[part][0], -step),
-            device_id_type=MESH,
-        )
-
-    for step in STEPS:
+            device_id=peer(ORDERS[part][0], origin - step),
+            device_id_type=MESH,
+        )
+
+    for step in (1, 3):
         for part in range(3):
             table_copy(part, step).start()
-    for step in STEPS:
-        for part in range(3):
-            phase0(part, step).start()
+    for first_half in (True, False):
+        for step in (1, 3):
+            for part in range(3):
+                phase0(part, step, RELAYED[step] if first_half else 1 - RELAYED[step]).start()
 
     other_weights = [
         pltpu.make_async_remote_copy(
@@ -198,9 +229,11 @@
             src, dst = mid_ref.at[group, step, :, :, here], landed.at[group, step, :, :, here]
             target = (order[2], -step)
         elif phase == 2:
+            here = back_cols(part)
             src, dst = landed.at[group, step, :, :, here], back_ref.at[group, :, step, :, here]
             target = (order[2], step)
         else:
+            here = back_cols(part)
             src, dst = back_ref.at[group, step, :, :, here], home_ref.at[group, step, :, :, here]
             target = (order[1], step)
         if step == 0:
@@ -246,13 +279,22 @@
             slot = (col & 3) + group * SLOTS
             mixes[group, part] = jnp.where((found == slot.astype(F32)) & mine, scale, 0.0).astype(BF16)
 
+    for part in range(3):
+        table_copy(part, 1).wait_recv()
+        table_copy(part, 2).start()
+    for part in range(3):
+        for step in (1, 3):
+            phase0(part, step, RELAYED[step]).wait_recv()
+            relay0(part, step).start()
     own_rows.wait()
     for part in range(3):
-        for step in STEPS:
-            table_copy(part, step).wait()
-    for part in range(3):
-        for step in STEPS:
-            phase0(part, step).wait()
+        table_copy(part, 3).wait_recv()
+        table_copy(part, 2).wait_recv()
+    for part in range(3):
+        for step in (1, 3):
+            phase0(part, step, 1 - RELAYED[step]).wait_recv()
+        for step in (1, 3):
+            relay0(part, step).wait_recv()
         gather(0, part)
         start(0, 0, part)
     for part in range(3):
@@ -267,6 +309,13 @@
         start(0, 2, part)
     for part in range(3):
         mix_tables(part)
+    for part in range(3):
+        for step in STEPS:
+            table_copy(part, step).wait_send()
+        for step in (1, 3):
+            phase0(part, step, 0).wait_send()
+            phase0(part, step, 1).wait_send()
+            relay0(part, step).wait_send()
     for part in range(3):
         finish(0, 1, part)
         start(1, 1, part)
@@ -293,7 +342,7 @@
             hidden[:, those] = (gate / (1.0 + jnp.exp(-gate)) * upper).astype(BF16)
 
     def outer(group, part):
-        first, size = PARTS[part]
+        first, size = BACK_PARTS[part]
         source = hidden
         if part:
             turned[...] = jnp.dot(
@@ -317,18 +366,18 @@
             for part in range(3):
                 finish(0, 2, part)
                 start(1, 2, part)
-        else:
+        for part in range(3):
+            outer(group, part)
+            start(2, group, part)
+        if group:
             for part in range(3):
                 finish(2, group - 1, part)
                 start(3, group - 1, part)
-        for part in range(3):
-            outer(group, part)
-            start(2, group, part)
 
     def load(group, part, step):
         return pltpu.make_async_copy(
-            home_ref.at[group, step, :, :, cols(part)],
-            packed.at[group, step, :, :, cols(part)],
+            home_ref.at[group, step, :, :, back_cols(part)],
+            packed.at[group, step, :, :, back_cols(part)],
             load_sem.at[group, part, step],
         )
 
@@ -338,31 +387,42 @@
             load(group, part, step).start()
 
     def mix(group, part):
-        first, size = PARTS[part]
+        here = back_cols(part)
         for step in STEPS:
             load(group, part, step).wait()
-        rows = packed[group, :, :, :, first : first + size].reshape(ROWS, size)
+        rows = packed[group, :, :, :, here].reshape(ROWS, BACK_PARTS[part][1])
         total = jnp.dot(mixes[group, part], rows, preferred_element_type=F32)
         if group:
-            total = total + mixed[:, first : first + size]
+            total = total + mixed[:, here]
+        mixed[:, here] = total
         if group == GROUPS - 1:
-            lines[:, first : first + size] = total.astype(BF16)
-        else:
-            mixed[:, first : first + size] = total
-
-    def phase5(part, step):
-        src = lines.at[pl.ds(step * TOK, TOK), cols(part)]
-        dst = sums.at[step, :, cols(part)]
-        if step == 0:
-            return pltpu.make_async_copy(src, dst, x_sem.at[1 + part])
+            lines[:, here] = total.astype(BF16)
+
+    def relay5(part, step):
+        here = half_cols(BACK_PARTS, part, RELAYED[step])
         return pltpu.make_async_remote_copy(
-            src_ref=src,
-            dst_ref=dst,
-            send_sem=end_send.at[1, part, step],
-            recv_sem=end_recv.at[1, part, step],
+            src_ref=lines.at[pl.ds(2 * TOK, TOK), here],
+            dst_ref=passing.at[:, here],
+            send_sem=end_send.at[2, part, step],
+            recv_sem=end_recv.at[2, part, step],
             device_id=peer(ORDERS[part][0], step),
             device_id_type=MESH,
         )
+
+    def phase5(part, step, half):
+        here = half_cols(BACK_PARTS, part, half)
+        return pltpu.make_async_remote_copy(
+            src_ref=lines.at[pl.ds(step * TOK, TOK), here],
+            dst_ref=sums.at[(step + 1) // 2, :, here],
+            send_sem=end_send.at[half, part, step],
+            recv_sem=end_recv.at[half, part, step],
+            device_id=peer(ORDERS[part][0], step),
+            device_id_type=MESH,
+        )
+
+    def own5(part):
+        here = back_cols(part)
+        return pltpu.make_async_copy(lines.at[pl.ds(0, TOK), here], sums.at[0, :, here], x_sem.at[1 + part])
 
     for part in range(3):
         bring(0, part)
@@ -378,11 +438,24 @@
     for part in range(3):
         bring(2, part)
         mix(2, part)
-        for step in STEPS + (0,):
-            phase5(part, step).start()
-    for part in range(3):
-        for step in STEPS + (0,):
-            phase5(part, step).wait()
+        for step in (1, 3):
+            relay5(part, step).start()
+        for step in (1, 3):
+            phase5(part, step, 1 - RELAYED[step]).start()
+        own5(part).start()
+    for part in range(3):
+        for step in (1, 3):
+            here = half_cols(BACK_PARTS, part, RELAYED[step])
+            these = slice(step * TOK, (step + 1) * TOK)
+            relay5(part, step).wait_recv()
+            lines[these, here] = (mixed[these, here] + passing[:, here].astype(F32)).astype(BF16)
+            phase5(part, step, RELAYED[step]).start()
+    for part in range(3):
+        own5(part).wait()
+        for step in (1, 3):
+            relay5(part, step).wait_send()
+            phase5(part, step, 0).wait()
+            phase5(part, step, 1).wait()
 
 
 def on_device(tokens, routes, gate_fixed, w_gate, w_up, w_down):
@@ -392,11 +465,12 @@
     dma = pltpu.SemaphoreType.DMA
     sums, _, _, _ = pl.pallas_call(
         kernel,
-        out_shape=(jax.ShapeDtypeStruct((SIDE, TOK, WIDTH), BF16), big, big, big),
+        out_shape=(jax.ShapeDtypeStruct((3, TOK, WIDTH), BF16), big, big, big),
         in_specs=[hbm, vmem, vmem, hbm, hbm, hbm],
         out_specs=(hbm, hbm, hbm, hbm),
         scratch_shapes=[
             pltpu.VMEM((SIDE * TOK, WIDTH), BF16),
+            pltpu.VMEM((TOK, WIDTH), BF16),
             pltpu.VMEM((3, SIDE * TOK, 2 * EXPERTS), BF16),
             pltpu.VMEM((GROUPS, SIDE, SIDE, BLOCK, WIDTH), BF16),
             pltpu.VMEM((GROUPS, SIDE, SIDE, BLOCK, WIDTH), BF16),
@@ -409,8 +483,10 @@
             pltpu.VMEM((2, HALF, WIDTH), BF16),
             dma((4, GROUPS, 3, SIDE)),
             dma((4, GROUPS, 3, SIDE)),
-            dma((2, 3, SIDE)),
-            dma((2, 3, SIDE)),
+            dma((3, 3, SIDE)),
+            dma((3, 3, SIDE)),
+            dma((3, 3, SIDE)),
+            dma((3, 3, SIDE)),
             dma((3, SIDE)),
             dma((3, SIDE)),
             dma((3,)),

time: 135 us -> 128 us (0.948)
  Pallas kernels: 131 us -> 125 us
    pallas_call x1, Pallas kernels: 131 us -> 125 us  [on_device(): pl.pallas_call(kernel, out_shape=(jax.ShapeDtypeStruct((3, TOK, WIDTH), B...]
where the time goes in v1:
time: 128 us
  Pallas kernels  125 us (98%)
  other arithmetic  2.61 us (2%)
    pallas_call x1, Pallas kernels, on_device(): pl.pallas_call(kernel, out_shape=(jax.ShapeDtypeStruct((3, TOK, WIDTH), B...  125 us
    reduce_sum x1, other arithmetic, on_device(): return jnp.sum(sums.astype(F32), axis=0).astype(BF16)  2.61 us

profile of v1, /device:TPU:0, one launch (start us, length us, event | category | flops | bytes accessed | tf_op | source)
XLA Modules:
  0.0 127.8 jit_solution(5165022257894562927)
XLA Ops:
  0.0 125.2 %moe.1 = (bf16[3,64,4096]{2,1,0:T(8,128)(2,1)}, bf16[3,4,4,16,4096]{4,3,2,1,0:T(8,128)(2,1)}, bf16[3,4,4,16,4096]{4,3,2,1,0:T(8,128)(2,1)}, bf16[3,4,4,16,4096]{4,3,2,1,0:T(8,128)(2,1)}) custom-call(bf16[64,4096]{1,0:T(8,128)(2,1)} %x_ref.1, s32[8,64]{1,0:T(8,128)} %bitcast.2, s32[8,64]{1,0:T(8,128)} %bitcast.3, bf16[1,4096,768]{2,1,0:T(8,128)(2,1)} %wg_hbm.1, ...), custom_call_target="tpu_custom_call" | custom-call | tf_op jit(solution)/shard_map/moe/pallas_call | solution.py:466
  125.2 2.6 %reduce_sum.12 = bf16[64,4096]{1,0:T(8,128)(2,1)} reduce(bf16[3,64,4096]{2,1,0:T(8,128)(2,1)} %get-tuple-element.6, bf16[]{:T(256)} %constant.2.clone.1), dimensions={0}, to_apply=%region_0.0 | reduce | flops 524288 | bytes 2097154 | tf_op jit(solution)/shard_map/reduce_sum | solution.py:504

commit v2 on v0

v2 whole, which is shorter than its diff:
```python
import jax
import jax.numpy as jnp
from jax import lax
from jax.experimental import pallas as pl
from jax.experimental.pallas import tpu as pltpu
from jax.sharding import PartitionSpec as P

MESH = pl.DeviceIdType.MESH
F32 = jnp.float32
BF16 = jnp.bfloat16

SIDE = 4
TOK = 64
TOP = 8
EXPERTS = 64
WIDTH = 4096
HALF = 768
GROUPS = 3
SLOTS = 4
BLOCK = SIDE * SLOTS
ROWS = SIDE * SIDE * BLOCK

PARTS = ((0, 1408), (1408, 1408), (2816, 1280))
BACK_PARTS = ((0, 1280), (1280, 1408), (2688, 1408))
ORDERS = ("yxz", "xzy", "zyx")
STEPS = (1, 3, 2)
CHUNK = 256


def nt(left, right):
    return lax.dot_general(left, right, (((1,), (1,)), ((), ())), preferred_element_type=F32)


def iota(shape, dim):
    return lax.broadcasted_iota(jnp.int32, shape, dim)


def ones_where(condition):
    return jnp.where(condition, 1.0, 0.0).astype(BF16)


def cols(part):
    return pl.ds(PARTS[part][0], PARTS[part][1])


def back_cols(part):
    return pl.ds(BACK_PARTS[part][0], BACK_PARTS[part][1])


RELAYED = {1: 0, 3: 1}


def stretch(parts, part, rest):
    first, size = parts[part]
    cut = 768 if parts is PARTS else size - 384
    return (first + cut, size - cut) if rest else (first, cut)


def stretch_cols(parts, part, rest):
    return pl.ds(*stretch(parts, part, rest))


def half_cols(parts, part, rest, half):
    first, size = stretch(parts, part, rest)
    cut = (size // 2 + 127) // 128 * 128
    return pl.ds(first + cut, size - cut) if half else pl.ds(first, cut)


def turn_matrix(forward):
    row = iota((ROWS, ROWS), 0)
    if forward:
        source = ((row >> 2) & 3) * 64 + (row >> 6) * 16 + ((row >> 4) & 3) * 4 + (row & 3)
    else:
        source = ((row >> 4) & 3) * 64 + ((row >> 2) & 3) * 16 + (row >> 6) * 4 + (row & 3)
    return ones_where(source == iota((ROWS, ROWS), 1))


def kernel(
    x_ref,
    routes_hbm,
    gate_hbm,
    wg_hbm,
    wu_hbm,
    wd_hbm,
    sums,
    mid_ref,
    back_ref,
    home_ref,
    routes_ref,
    gate_ref,
    lines,
    passing,
    last,
    tables,
    packed,
    landed,
    hidden,
    turned,
    mixes,
    mixed,
    wg,
    wu,
    wd,
    hop_send,
    hop_recv,
    start_send,
    first_recv,
    start_recv,
    pass_recv,
    end_sem,
    tab_sem,
    w_send,
    w_recv,
    w_local,
    own_sem,
    load_sem,
    x_sem,
):
    row = lax.axis_index("expert")
    at = {"y": lax.axis_index("dp"), "x": row // 8, "z": (row // 2) % 4}
    core = row % 2

    def device(where, which):
        return (where["y"], (where["x"] * 4 + where["z"]) * 2 + which)

    def peer(axis, shift):
        where = dict(at)
        where[axis] = (at[axis] + shift) % SIDE
        return device(where, core)

    partner = device(at, 1 - core)

    barrier = pltpu.get_barrier_semaphore()
    for step in (1, 3):
        for axis in "yxz":
            pl.semaphore_signal(barrier, inc=1, device_id=peer(axis, step), device_id_type=MESH)
    pl.semaphore_signal(barrier, inc=1, device_id=partner, device_id_type=MESH)

    def wait_bytes(ref, sem):
        pltpu.make_async_copy(ref, ref, sem).wait()

    own_rows = pltpu.make_async_copy(x_ref, lines.at[pl.ds(0, TOK)], x_sem.at[0])
    own_choices = [
        pltpu.make_async_copy(routes_hbm, routes_ref, x_sem.at[1]),
        pltpu.make_async_copy(gate_hbm, gate_ref, x_sem.at[2]),
    ]
    for copy in own_choices + [own_rows]:
        copy.start()
    own_weights = [
        pltpu.make_async_copy(src.at[0], dst.at[0], w_local.at[index])
        for index, (src, dst) in enumerate(((wg_hbm, wg), (wu_hbm, wu), (wd_hbm, wd)))
    ]

    pl.semaphore_wait(barrier, 7)

    def phase0(part, step, rest, half):
        here = half_cols(PARTS, part, rest, half)
        return pltpu.make_async_remote_copy(
            src_ref=x_ref.at[:, here],
            dst_ref=lines.at[pl.ds(step * TOK, TOK), here],
            send_sem=start_send.at[0],
            recv_sem=first_recv.at[rest, part, step // 2] if half == RELAYED[step] else start_recv.at[rest, part],
            device_id=peer(ORDERS[part][0], -step),
            device_id_type=MESH,
        )

    def relay0(part, step, rest):
        here = half_cols(PARTS, part, rest, RELAYED[step])
        return pltpu.make_async_remote_copy(
            src_ref=lines.at[pl.ds(step * TOK, TOK), here],
            dst_ref=lines.at[pl.ds(2 * TOK, TOK), here],
            send_sem=start_send.at[0],
            recv_sem=start_recv.at[rest, part],
            device_id=peer(ORDERS[part][0], -step),
            device_id_type=MESH,
        )

    def table_copy(part, step):
        origin = 1 if step == 2 else 0
        return pltpu.make_async_remote_copy(
            src_ref=tables.at[part, pl.ds(origin * TOK, TOK)],
            dst_ref=tables.at[part, pl.ds(step * TOK, TOK)],
            send_sem=tab_sem.at[0],
            recv_sem=tab_sem.at[1 if step == 1 else 2],
            device_id=peer(ORDERS[part][0], origin - step),
            device_id_type=MESH,
        )

    def start_tokens(rest, relayed):
        for step in (1, 3):
            for part in range(3):
                phase0(part, step, rest, RELAYED[step] if relayed else 1 - RELAYED[step]).start()

    def pass_on(rest):
        for part in range(3):
            for step in (1, 3):
                phase0(part, step, rest, RELAYED[step]).wait_recv()
                relay0(part, step, rest).start()

    start_tokens(0, True)
    start_tokens(0, False)
    for copy in own_choices:
        copy.wait()

    quant = gate_ref[...].astype(F32)
    weight = quant / jnp.sum(quant, axis=0, keepdims=True)
    named = jnp.zeros((EXPERTS, TOK), F32)
    share = jnp.zeros((EXPERTS, TOK), F32)
    for k in range(TOP):
        hit = routes_ref[k : k + 1, :] == iota((EXPERTS, TOK), 0)
        named = named + jnp.where(hit, 1.0, 0.0)
        share = share + jnp.where(hit, weight[k : k + 1, :], 0.0)
    earlier = ones_where(iota((TOK, TOK), 0) < iota((TOK, TOK), 1))
    before = jnp.dot(named.astype(BF16), earlier, preferred_element_type=F32)
    slots = jnp.where(named > 0.5, before, -1.0)
    own_table = jnp.concatenate([slots, share], axis=0).T.astype(BF16)
    for part in range(3):
        tables[part, 0:TOK, :] = own_table

    for step in (1, 3):
        for part in range(3):
            table_copy(part, step).start()
    start_tokens(1, True)

    other_weights = [
        pltpu.make_async_remote_copy(
            src_ref=src.at[0],
            dst_ref=dst.at[1],
            send_sem=w_send.at[index],
            recv_sem=w_recv.at[index],
            device_id=partner,
            device_id_type=MESH,
        )
        for index, (src, dst) in enumerate(((wg_hbm, wg), (wu_hbm, wu), (wd_hbm, wd)))
    ]

    def chosen(part):
        index = iota((ROWS, EXPERTS), 0)
        a, b, c = (at[axis] for axis in ORDERS[part])
        where = dict(zip(ORDERS[part], (a, (b - (index >> 6)) & 3, (c - ((index >> 4) & 3)) & 3)))
        expert = where["y"] * 16 + where["x"] * 4 + where["z"]
        return ones_where(expert == iota((ROWS, EXPERTS), 1))

    def ends(phase, group, step, here):
        if phase == 0:
            return packed.at[group, step, :, :, here], mid_ref.at[group, :, step, :, here]
        if phase == 1:
            return mid_ref.at[group, step, :, :, here], landed.at[group, step, :, :, here]
        if phase == 2:
            return landed.at[group, step, :, :, here], back_ref.at[group, :, step, :, here]
        if group == GROUPS - 1:
            return back_ref.at[group, step, :, :, here], last.at[step, :, :, here]
        return back_ref.at[group, step, :, :, here], home_ref.at[group, step, :, :, here]

    def part_cols(phase, part, rest):
        parts = PARTS if phase < 2 else BACK_PARTS
        return pl.ds(*(parts[part] if rest is None else stretch(parts, part, rest)))

    def start(phase, group, part, rest=None):
        axis = ORDERS[part][1 if phase in (0, 3) else 2]
        for step in STEPS:
            src, dst = ends(phase, group, step, part_cols(phase, part, rest))
            pltpu.make_async_remote_copy(
                src_ref=src,
                dst_ref=dst,
                send_sem=hop_send.at[phase, group if phase == 0 else 0],
                recv_sem=hop_recv.at[phase, GROUPS if rest else group, part],
                device_id=peer(axis, step if phase > 1 else -step),
                device_id_type=MESH,
            ).start()

    def finish(phase, group, part, rest=None):
        _, dst = ends(phase, group, pl.ds(1, SIDE - 1), part_cols(phase, part, rest))
        wait_bytes(dst, hop_recv.at[phase, GROUPS if rest else group, part])

    def own_hop(phase, group):
        src, dst = ends(phase, group, 0, pl.ds(0, WIDTH))
        if phase == 3 and group < GROUPS - 1:
            dst = packed.at[group, 0]
        return pltpu.make_async_copy(src, dst, own_sem.at[phase, group])

    def start_own(phase, group):
        own_hop(phase, group).start()

    def finish_own(phase, group):
        own_hop(phase, group).wait()

    def finish_all(phase, group):
        finish_own(phase, group)
        for part in range(3):
            finish(phase, group, part)

    def gather(group, part, rest=None):
        first, size = PARTS[part] if rest is None else stretch(PARTS, part, rest)
        found = nt(chosen(part), tables[part, :, 0:EXPERTS])
        row = iota((ROWS, SIDE * TOK), 0)
        slot = (row & 3) + group * SLOTS
        holder = iota((ROWS, SIDE * TOK), 1) >> 6
        pick = ones_where((found == slot.astype(F32)) & (holder == ((row >> 2) & 3)))
        rows = jnp.dot(pick, lines[:, first : first + size], preferred_element_type=F32)
        packed[group, :, :, :, first : first + size] = rows.astype(BF16).reshape(SIDE, SIDE, BLOCK, size)

    def mix_tables(part):
        select = chosen(part)
        found = nt(tables[part, :, 0:EXPERTS], select)
        scale = nt(tables[part, :, EXPERTS : 2 * EXPERTS], select)
        col = iota((SIDE * TOK, ROWS), 1)
        mine = (iota((SIDE * TOK, ROWS), 0) >> 6) == ((col >> 2) & 3)
        for group in range(GROUPS):
            slot = (col & 3) + group * SLOTS
            mixes[group, part] = jnp.where((found == slot.astype(F32)) & mine, scale, 0.0).astype(BF16)

    wait_bytes(tables.at[:, pl.ds(0, TOK)], tab_sem.at[1])
    for part in range(3):
        table_copy(part, 2).start()
    pass_on(0)
    start_tokens(1, False)
    for copy in own_weights + other_weights:
        copy.start()
    own_rows.wait()
    pass_on(1)
    wait_bytes(tables.at[:, pl.ds(0, 2 * TOK)], tab_sem.at[2])
    for rest in range(2):
        for part in range(3):
            here = stretch_cols(PARTS, part, rest)
            wait_bytes(lines.at[pl.ds(0, 2 * TOK), here], start_recv.at[rest, part])
            gather(0, part, rest)
            start(0, 0, part, rest)
    start_own(0, 0)
    for part in range(3):
        gather(1, part)
        start(0, 1, part)
    start_own(0, 1)
    for part in range(3):
        gather(2, part)
    finish_own(0, 0)
    for part in range(3):
        finish(0, 0, part, 0)
        finish(0, 0, part, 1)
        start(1, 0, part)
    start_own(1, 0)
    for part in range(3):
        start(0, 2, part)
    start_own(0, 2)
    for part in range(3):
        mix_tables(part)
    wait_bytes(tables.at[:, pl.ds(0, 3 * TOK)], tab_sem.at[0])
    wait_bytes(lines.at[pl.ds(0, 3 * TOK)], start_send.at[0])
    finish_own(0, 1)
    for part in range(3):
        finish(0, 1, part)
        start(1, 1, part)
    start_own(1, 1)

    def arrange(group):
        for part in range(3):
            first, size = PARTS[part]
            rows = landed[group, :, :, :, first : first + size]
            if part:
                rows = rows.reshape(ROWS, size)
                rows = jnp.dot(turn_matrix(part == 1), rows, preferred_element_type=F32)
                rows = rows.astype(BF16).reshape(SIDE, SIDE, BLOCK, size)
            packed[group, :, :, :, first : first + size] = rows

    def inner(group):
        @pl.loop(0, 2 * HALF // CHUNK)
        def _(index):
            side = index // (HALF // CHUNK)
            these = pl.ds(pl.multiple_of((index % (HALF // CHUNK)) * CHUNK, CHUNK), CHUNK)
            those = pl.ds(pl.multiple_of(index * CHUNK, CHUNK), CHUNK)
            rows = packed[group].reshape(ROWS, WIDTH)
            gate = jnp.dot(rows, wg[side, :, these], preferred_element_type=F32)
            upper = jnp.dot(rows, wu[side, :, these], preferred_element_type=F32)
            hidden[:, those] = (gate / (1.0 + jnp.exp(-gate)) * upper).astype(BF16)

    def outer(group, part):
        first, size = BACK_PARTS[part]
        source = hidden
        if part:
            turned[...] = jnp.dot(
                turn_matrix(part == 2), hidden[...], preferred_element_type=F32
            ).astype(BF16)
            source = turned
        for begin in range(first, first + size, CHUNK):
            end = min(begin + CHUNK, first + size)
            total = jnp.dot(source[:, :HALF], wd[0, :, begin:end], preferred_element_type=F32)
            total = total + jnp.dot(source[:, HALF:], wd[1, :, begin:end], preferred_element_type=F32)
            landed[group, :, :, :, begin:end] = total.astype(BF16).reshape(SIDE, SIDE, BLOCK, end - begin)

    for copy in own_weights + other_weights:
        copy.wait()

    for group in range(GROUPS):
        finish_all(1, group)
        wait_bytes(packed.at[group, pl.ds(1, SIDE - 1)], hop_send.at[0, group])
        arrange(group)
        inner(group)
        if group == 0:
            finish_own(0, 2)
            for part in range(3):
                finish(0, 2, part)
                start(1, 2, part)
            start_own(1, 2)
        for part in range(3):
            outer(group, part)
            start(2, group, part)
        start_own(2, group)
        if group:
            finish_own(2, group - 1)
            for part in range(3):
                finish(2, group - 1, part)
                start(3, group - 1, part)
            start_own(3, group - 1)

    def load(group, part):
        here = back_cols(part)
        steps = pl.ds(1, SIDE - 1)
        return pltpu.make_async_copy(
            home_ref.at[group, steps, :, :, here],
            packed.at[group, steps, :, :, here],
            load_sem.at[group, part],
        )

    def mix(group):
        for part in range(3):
            finish(3, group, part)
            load(group, part).start()
        finish_own(3, group)
        for part in range(3):
            load(group, part).wait()
            here = back_cols(part)
            rows = packed[group, :, :, :, here].reshape(ROWS, BACK_PARTS[part][1])
            total = jnp.dot(mixes[group, part], rows, preferred_element_type=F32)
            if group:
                total = total + mixed[:, here]
            mixed[:, here] = total

    def mix_last(part, rest):
        here = stretch_cols(BACK_PARTS, part, rest)
        rows = last[:, :, :, here].reshape(ROWS, here.size)
        total = jnp.dot(mixes[GROUPS - 1, part], rows, preferred_element_type=F32) + mixed[:, here]
        mixed[:, here] = total
        lines[:, here] = total.astype(BF16)

    def relay5(part, step, rest):
        here = half_cols(BACK_PARTS, part, rest, RELAYED[step])
        return pltpu.make_async_remote_copy(
            src_ref=lines.at[pl.ds(2 * TOK, TOK), here],
            dst_ref=passing.at[:, here],
            send_sem=end_sem.at[0],
            recv_sem=pass_recv.at[rest, part, step // 2],
            device_id=peer(ORDERS[part][0], step),
            device_id_type=MESH,
        )

    def phase5(part, step, rest, half):
        here = half_cols(BACK_PARTS, part, rest, half)
        return pltpu.make_async_remote_copy(
            src_ref=lines.at[pl.ds(step * TOK, TOK), here],
            dst_ref=sums.at[(step + 1) // 2, :, here],
            send_sem=end_sem.at[0],
            recv_sem=end_sem.at[1],
            device_id=peer(ORDERS[part][0], step),
            device_id_type=MESH,
        )

    mix(0)
    finish_own(2, GROUPS - 1)
    for rest in range(2):
        for part in range(3):
            if rest == 0:
                finish(2, GROUPS - 1, part)
            start(3, GROUPS - 1, part, rest)
    start_own(3, GROUPS - 1)
    mix(1)
    finish_own(3, GROUPS - 1)
    for rest in range(2):
        for part in range(3):
            finish(3, GROUPS - 1, part, rest)
            mix_last(part, rest)
            for step in (1, 3):
                relay5(part, step, rest).start()
        for part in range(3):
            for step in (1, 3):
                phase5(part, step, rest, 1 - RELAYED[step]).start()
        for part in range(3):
            for step in (1, 3):
                here = half_cols(BACK_PARTS, part, rest, RELAYED[step])
                these = slice(step * TOK, (step + 1) * TOK)
                relay5(part, step, rest).wait_recv()
                lines[these, here] = (mixed[these, here] + passing[:, here].astype(F32)).astype(BF16)
                phase5(part, step, rest, RELAYED[step]).start()
    own5 = pltpu.make_async_copy(lines.at[pl.ds(0, TOK)], sums.at[0], x_sem.at[0])
    own5.start()
    wait_bytes(mid_ref.at[:, pl.ds(1, SIDE - 1)], hop_send.at[1, 0])
    wait_bytes(landed.at[:, pl.ds(1, SIDE - 1)], hop_send.at[2, 0])
    wait_bytes(back_ref.at[:, pl.ds(1, SIDE - 1)], hop_send.at[3, 0])
    own5.wait()
    wait_bytes(lines.at[pl.ds(0, 3 * TOK)], end_sem.at[0])
    wait_bytes(sums.at[pl.ds(1, 2)], end_sem.at[1])


def on_device(tokens, routes, gate_fixed, w_gate, w_up, w_down):
    big = jax.ShapeDtypeStruct((GROUPS, SIDE, SIDE, BLOCK, WIDTH), BF16)
    hbm = pl.BlockSpec(memory_space=pltpu.HBM)
    dma = pltpu.SemaphoreType.DMA
    sums, _, _, _ = pl.pallas_call(
        kernel,
        out_shape=(jax.ShapeDtypeStruct((3, TOK, WIDTH), BF16), big, big, big),
        in_specs=[hbm] * 6,
        out_specs=(hbm, hbm, hbm, hbm),
        scratch_shapes=[
            pltpu.VMEM((TOP, TOK), jnp.int32),
            pltpu.VMEM((TOP, TOK), jnp.int32),
            pltpu.VMEM((SIDE * TOK, WIDTH), BF16),
            pltpu.VMEM((TOK, WIDTH), BF16),
            pltpu.VMEM((SIDE, SIDE, BLOCK, WIDTH), BF16),
            pltpu.VMEM((3, SIDE * TOK, 2 * EXPERTS), BF16),
            pltpu.VMEM((GROUPS, SIDE, SIDE, BLOCK, WIDTH), BF16),
            pltpu.VMEM((GROUPS, SIDE, SIDE, BLOCK, WIDTH), BF16),
            pltpu.VMEM((ROWS, 2 * HALF), BF16),
            pltpu.VMEM((ROWS, 2 * HALF), BF16),
            pltpu.VMEM((GROUPS, 3, SIDE * TOK, ROWS), BF16),
            pltpu.VMEM((SIDE * TOK, WIDTH), F32),
            pltpu.VMEM((2, WIDTH, HALF), BF16),
            pltpu.VMEM((2, WIDTH, HALF), BF16),
            pltpu.VMEM((2, HALF, WIDTH), BF16),
            dma((4, GROUPS)),
            dma((4, GROUPS + 1, 3)),
            dma((1,)),
            dma((2, 3, 2)),
            dma((2, 3)),
            dma((2, 3, 2)),
            dma((2,)),
            dma((3,)),
            dma((3,)),
            dma((3,)),
            dma((3,)),
            dma((4, GROUPS)),
            dma((2, 3)),
            dma((3,)),
        ],
        compiler_params=pltpu.CompilerParams(
            collective_id=0, has_side_effects=True, vmem_limit_bytes=67043328
        ),
        name="moe",
    )(tokens, routes.T, gate_fixed.T, w_gate, w_up, w_down)
    return jnp.sum(sums.astype(F32), axis=0).astype(BF16)


def solution(mesh):
    split = P(("dp", "expert"), None)
    placed = (split, split, split) + (P(("dp", "expert"), None, None),) * 3
    return jax.shard_map(on_device, mesh=mesh, in_specs=placed, out_specs=split, check_vma=False)
```

time: 135 us -> 124 us (0.919)
  Pallas kernels: 131 us -> 121 us
    pallas_call x1, Pallas kernels: 131 us -> 121 us  [on_device(): pl.pallas_call(kernel, out_shape=(jax.ShapeDtypeStruct((3, TOK, WIDTH), B...]
where the time goes in v2:
time: 124 us
  Pallas kernels  121 us (98%)
  other arithmetic  2.61 us (2%)
    pallas_call x1, Pallas kernels, on_device(): pl.pallas_call(kernel, out_shape=(jax.ShapeDtypeStruct((3, TOK, WIDTH), B...  121 us
    reduce_sum x1, other arithmetic, on_device(): return jnp.sum(sums.astype(F32), axis=0).astype(BF16)  2.61 us

profile of v2, /device:TPU:0, one launch (start us, length us, event | category | flops | bytes accessed | tf_op | source)
XLA Modules:
  0.0 124.0 jit_solution(14179766293849013618)
XLA Ops:
  0.0 121.3 %moe.1 = (bf16[3,64,4096]{2,1,0:T(8,128)(2,1)}, bf16[3,4,4,16,4096]{4,3,2,1,0:T(8,128)(2,1)}, bf16[3,4,4,16,4096]{4,3,2,1,0:T(8,128)(2,1)}, bf16[3,4,4,16,4096]{4,3,2,1,0:T(8,128)(2,1)}) custom-call(bf16[64,4096]{1,0:T(8,128)(2,1)} %x_ref.1, s32[8,64]{1,0:T(8,128)} %bitcast.2, s32[8,64]{1,0:T(8,128)} %bitcast.3, bf16[1,4096,768]{2,1,0:T(8,128)(2,1)} %wg_hbm.1, ...), custom_call_target="tpu_custom_call" | custom-call | tf_op jit(solution)/shard_map/moe/pallas_call | solution.py:507
  121.4 2.6 %reduce_sum.12 = bf16[64,4096]{1,0:T(8,128)(2,1)} reduce(bf16[3,64,4096]{2,1,0:T(8,128)(2,1)} %get-tuple-element.6, bf16[]{:T(256)} %constant.2.clone.1), dimensions={0}, to_apply=%region_0.0 | reduce | flops 524288 | bytes 2097154 | tf_op jit(solution)/shard_map/reduce_sum | solution.py:548

commit v3 on v2

--- a/solution.py
+++ b/solution.py
@@ -480,9 +480,11 @@
             mix_last(part, rest)
             for step in (1, 3):
                 relay5(part, step, rest).start()
-        for part in range(3):
-            for step in (1, 3):
-                phase5(part, step, rest, 1 - RELAYED[step]).start()
+        if rest == 0:
+            for part in range(3):
+                for step in (1, 3):
+                    phase5(part, step, rest, 1 - RELAYED[step]).start()
+    for rest in range(2):
         for part in range(3):
             for step in (1, 3):
                 here = half_cols(BACK_PARTS, part, rest, RELAYED[step])
@@ -490,6 +492,10 @@
                 relay5(part, step, rest).wait_recv()
                 lines[these, here] = (mixed[these, here] + passing[:, here].astype(F32)).astype(BF16)
                 phase5(part, step, rest, RELAYED[step]).start()
+        if rest == 0:
+            for part in range(3):
+                for step in (1, 3):
+                    phase5(part, step, 1, 1 - RELAYED[step]).start()
     own5 = pltpu.make_async_copy(lines.at[pl.ds(0, TOK)], sums.at[0], x_sem.at[0])
     own5.start()
     wait_bytes(mid_ref.at[:, pl.ds(1, SIDE - 1)], hop_send.at[1, 0])

time: 124 us -> 121 us (0.976)
  Pallas kernels: 121 us -> 118 us
    pallas_call x1, Pallas kernels: 121 us -> 118 us  [on_device(): pl.pallas_call(kernel, out_shape=(jax.ShapeDtypeStruct((3, TOK, WIDTH), B...]
where the time goes in v3:
time: 121 us; the launch traced here: 120 us
  Pallas kernels  118 us (98%)
  other arithmetic  2.61 us (2%)
    pallas_call x1, Pallas kernels, on_device(): pl.pallas_call(kernel, out_shape=(jax.ShapeDtypeStruct((3, TOK, WIDTH), B...  118 us
    reduce_sum x1, other arithmetic, on_device(): return jnp.sum(sums.astype(F32), axis=0).astype(BF16)  2.61 us

profile of v3, /device:TPU:0, one launch (start us, length us, event | category | flops | bytes accessed | tf_op | source)
XLA Modules:
  0.0 120.5 jit_solution(10990303585324467482)
XLA Ops:
  0.0 117.9 %moe.1 = (bf16[3,64,4096]{2,1,0:T(8,128)(2,1)}, bf16[3,4,4,16,4096]{4,3,2,1,0:T(8,128)(2,1)}, bf16[3,4,4,16,4096]{4,3,2,1,0:T(8,128)(2,1)}, bf16[3,4,4,16,4096]{4,3,2,1,0:T(8,128)(2,1)}) custom-call(bf16[64,4096]{1,0:T(8,128)(2,1)} %x_ref.1, s32[8,64]{1,0:T(8,128)} %bitcast.2, s32[8,64]{1,0:T(8,128)} %bitcast.3, bf16[1,4096,768]{2,1,0:T(8,128)(2,1)} %wg_hbm.1, ...), custom_call_target="tpu_custom_call" | custom-call | tf_op jit(solution)/shard_map/moe/pallas_call | solution.py:513
  117.9 2.6 %reduce_sum.12 = bf16[64,4096]{1,0:T(8,128)(2,1)} reduce(bf16[3,64,4096]{2,1,0:T(8,128)(2,1)} %get-tuple-element.6, bf16[]{:T(256)} %constant.2.clone.1), dimensions={0}, to_apply=%region_0.0 | reduce | flops 524288 | bytes 2097154 | tf_op jit(solution)/shard_map/reduce_sum | solution.py:554
